TPU v7x, 128 devices: a whole 4x4x4 slice. The times are simulated.
128 devices in a mesh: ctx: 16 (over y_hi, x, core), vocab: 8 (over y_lo, z).
Axes of the slice: x: 4, y: 4 (y_hi: 2, y_lo: 2; y = y_hi * 2 + y_lo), z: 4, core: 2. Of those that a mesh axis runs over, the one named last changes fastest.
Arguments:
- block_query: bfloat16 [512, 6144], P('ctx', 'vocab'), may hold values from -16 to 16
- block_key: bfloat16 [512, 6144], P('ctx', 'vocab'), may hold values from -16 to 16
- block_value: bfloat16 [512, 6144], P('ctx', 'vocab'), may hold values from -6 to 6
- block_doc: int32 [512], P('ctx'), may hold values from 0 to 1, never falling along the last dimension, each value on 1 to 480 neighbouring positions
- token_query: bfloat16 [2048, 6144], P(('ctx', 'vocab')), may hold values from -16 to 16
- token_key: bfloat16 [2048, 6144], P(('ctx', 'vocab')), may hold values from -16 to 16
- token_value: bfloat16 [2048, 6144], P(('ctx', 'vocab')), may hold values from -600 to 600
- token_state: bfloat16 [2048, 6144], P(('ctx', 'vocab')), may hold values from -6 to 6
- norm_gain: float32 [6144], replicated, may hold values from 0.5 to 1.5
- head_weight: bfloat16 [6144, 131072], P(None, ('ctx', 'vocab')), may hold values from -128 to 128
- targets: int32 [2048], replicated, may hold values from 0 to 131071
Outputs:
- block_context: bfloat16 [512, 6144], P('ctx', 'vocab')
- token_prior: float32 [2048], P(('ctx', 'vocab'))
Inputs may be any that keep to these rules, and one draw needn't show every extreme that they name: block_doc never falls along the blocks; no document holds more than 480 blocks.
All inputs are finite; a program needn't handle non-finite values.
Results may differ from a plain program's by a relative error of at most 0.005.
Values may be sent and summed in bfloat16 or wider, within the bound.
No kernel may reach another device: no remote copies, remote signals or barrier semaphores. Data moves between devices by JAX's collectives and lax.ppermute only.
A program may use at most 128 MiB of HBM per device.

v0:
```python
import math
import jax
import jax.numpy as jnp
from jax import lax
from jax.sharding import Mesh
from jax.sharding import PartitionSpec as P

HEAD_DIM = 128
BLOCK_LEN = 4
CTX = ("ctx_0", "ctx_1", "ctx_2")
VOCAB = ("vocab_0", "vocab_1")
CTX_VOCAB = ("ctx_0", "ctx_1", "ctx_2", "vocab_0", "vocab_1")
big_negative = -1e30


def sent_to_all(value, axis):
    size = lax.axis_size(axis)
    return lax.all_to_all(
        jnp.broadcast_to(value[None], (size, *value.shape)), axis, 0, 0, tiled=True
    )


def joined_along(pieces, dim):
    pieces = jnp.moveaxis(pieces, 0, dim)
    shape = pieces.shape
    return pieces.reshape(*shape[:dim], shape[dim] * shape[dim + 1], *shape[dim + 2 :])


def gathered_copies(value, axis, dim):
    pieces = sent_to_all(value, axis)
    return joined_along(pieces, dim)


def all_in_one(value, axis):
    leaves = jax.tree.leaves(value)
    sequence = sorted(range(len(leaves)), key=lambda k: -leaves[k].size)
    width = (1, *leaves[sequence[0]].shape)[-1]
    lines = [
        jnp.pad(leaves[k].reshape(-1), (0, -leaves[k].size % width)).reshape(-1, width)
        for k in sequence
    ]
    both, at, found = (lax.all_gather(jnp.concatenate(lines), axis), 0, {})
    for k, line in zip(sequence, lines):
        share = both[:, at : at + len(line)].reshape(len(both), -1)
        found[k] = share[:, : leaves[k].size].reshape(-1, *leaves[k].shape)
        at += len(line)
    numbers = iter(range(len(leaves)))
    return jax.tree.map(lambda _: found[next(numbers)], value)


def merged_by_axis(value, axes, combine):
    for axis in axes:
        pieces = all_in_one(value, axis)
        value = jax.tree.map(lambda part: part[0], pieces)
        for k in range(1, lax.axis_size(axis)):
            value = combine(value, jax.tree.map(lambda part: part[k], pieces))
    return value


def local_decoder(context, token_query, token_key, token_value, token_state, norm_gain):
    scale = 1.0 / math.sqrt(HEAD_DIM)
    groups = context.shape[0]
    width = context.shape[1]
    head_total = width // HEAD_DIM
    shape = (groups, BLOCK_LEN, head_total, HEAD_DIM)
    prefix = context.reshape(groups, 1, head_total, HEAD_DIM)
    queries = token_query.reshape(shape)
    keys = jnp.concatenate([prefix, token_key.reshape(shape)], axis=1)
    values = jnp.concatenate([prefix, token_value.reshape(shape)], axis=1)
    scores = (
        jnp.einsum("bihd,bjhd->bhij", queries, keys, preferred_element_type=jnp.float32) * scale
    )
    allowed = (
        jnp.arange(BLOCK_LEN + 1, dtype=jnp.int32)[None, :]
        <= jnp.arange(BLOCK_LEN, dtype=jnp.int32)[:, None] + 1
    )
    scores = jnp.where(allowed, scores, -jnp.inf)
    highest = jnp.max(scores, axis=-1, keepdims=True)
    weights = jnp.exp(scores - highest)
    totals = jnp.sum(weights, axis=-1)
    mixed = jnp.einsum(
        "bhij,bjhd->bihd", weights.astype(jnp.bfloat16), values, preferred_element_type=jnp.float32
    )
    mixed = mixed / jnp.transpose(totals, (0, 2, 1))[..., None]
    summed = token_state.astype(jnp.float32) + mixed.reshape(groups * BLOCK_LEN, width)
    power = jnp.mean(summed * summed, axis=-1, keepdims=True)
    return (summed * lax.rsqrt(power + 1e-05) * norm_gain).astype(jnp.bfloat16)


def local(
    block_query,
    block_key,
    block_value,
    block_doc,
    token_query,
    token_key,
    token_value,
    token_state,
    norm_gain,
    head_weight,
    targets,
):
    local_rows = block_query.shape[0]
    head_count = block_query.shape[1] // HEAD_DIM
    scale = 1.0 / math.sqrt(HEAD_DIM)
    first_row = lax.axis_index(CTX) * local_rows
    queries = block_query.reshape(local_rows, head_count, HEAD_DIM)
    own_doc = block_doc.astype(jnp.bfloat16)
    query_places = first_row + jnp.arange(local_rows, dtype=jnp.int32)
    highest = jnp.full((local_rows, head_count), big_negative, jnp.float32)
    keys = lax.all_gather(block_key, CTX, axis=0, tiled=True)
    values = lax.all_gather(block_value, CTX, axis=0, tiled=True)
    docs = lax.all_gather(own_doc, CTX, axis=0, tiled=True)
    count = keys.shape[0]
    keys = keys.reshape(count, head_count, HEAD_DIM)
    values = values.reshape(count, head_count, HEAD_DIM)
    scores = jnp.einsum("qhd,khd->qhk", queries, keys, preferred_element_type=jnp.float32) * scale
    key_places = jnp.arange(count, dtype=jnp.int32)
    allowed = (query_places[:, None] >= key_places[None, :]) & (own_doc[:, None] == docs[None, :])
    allowed = allowed[:, None, :]
    newest = jnp.maximum(highest, jnp.max(jnp.where(allowed, scores, big_negative), axis=-1))
    weights = jnp.where(allowed, jnp.exp(scores - newest[..., None]), 0.0)
    totals = jnp.sum(weights, axis=-1)
    update = jnp.einsum(
        "qhk,khd->qhd", weights.astype(jnp.bfloat16), values, preferred_element_type=jnp.float32
    )
    mixed = update
    highest, totals, mixed = (newest, totals, mixed)
    block_context = (
        (mixed / totals[..., None]).reshape(local_rows, head_count * HEAD_DIM).astype(jnp.bfloat16)
    )
    grouped = lax.all_to_all(block_context, VOCAB, split_axis=0, concat_axis=1, tiled=True)
    hidden = local_decoder(grouped, token_query, token_key, token_value, token_state, norm_gain)
    vocab_cols = head_weight.shape[1]
    col_start = lax.axis_index(CTX_VOCAB) * vocab_cols
    columns = jnp.arange(vocab_cols, dtype=jnp.int32)
    group_states = gathered_copies(hidden, VOCAB, 0)
    piece = lax.all_gather(group_states, CTX, axis=0, tiled=True)
    logits = jnp.dot(piece, head_weight, preferred_element_type=jnp.float32)
    top = jnp.max(logits, axis=-1)
    mass = jnp.sum(jnp.exp(logits - top[:, None]), axis=-1)
    wanted = targets - col_start
    picked = jnp.sum(jnp.where(columns[None, :] == wanted[:, None], logits, 0.0), axis=1)
    peaks = top
    masses = mass
    picks = picked
    stats = (peaks, masses, picks)

    def combine(left, right):
        top = jnp.maximum(left[0], right[0])
        mass = left[1] * jnp.exp(left[0] - top) + right[1] * jnp.exp(right[0] - top)
        return (top, mass, left[2] + right[2])

    peaks, masses, picks = merged_by_axis(stats, CTX_VOCAB, combine)
    priors = picks - (peaks + jnp.log(masses))
    own_count = hidden.shape[0]
    token_prior = lax.dynamic_slice_in_dim(priors, lax.axis_index(CTX_VOCAB) * own_count, own_count)
    return (block_context, token_prior)


def solution(mesh):
    torus = Mesh(
        mesh.devices.reshape(2, 4, 2, 2, 4), ("ctx_0", "ctx_1", "ctx_2", "vocab_0", "vocab_1")
    )
    in_specs = (
        P(CTX, VOCAB),
        P(CTX, VOCAB),
        P(CTX, VOCAB),
        P(CTX),
        P(CTX_VOCAB, None),
        P(CTX_VOCAB, None),
        P(CTX_VOCAB, None),
        P(CTX_VOCAB, None),
        P(),
        P(None, CTX_VOCAB),
        P(),
    )
    out_specs = (P(CTX, VOCAB), P(CTX_VOCAB))
    return jax.shard_map(local, mesh=torus, in_specs=in_specs, out_specs=out_specs, check_vma=False)
```

profile of v0, /device:TPU:0, one launch (start us, length us, event | category | flops | bytes accessed | tf_op | source)
XLA Modules:
  0.0 360.8 jit_solution(2283637337288649313)
XLA Ops:
  7.2 0.8 convert_element_type.25
  8.0 1.2 dynamic-slice
  9.9 0.2 dynamic-update-slice
  10.1 38.1 %all-reduce = bf16[512]{0:T(512)(128)(2,1)S(1)} all-reduce(bf16[512]{0:T(512)(128)(2,1)S(1)} %dynamic-update-slice), channel_id=1, replica_groups=mesh['ctx_0'=2,'ctx_1'=4,'ctx_2'=2,'vocab_0'=2,'vocab_1'=4] {'ctx_0','ct..., use_global_device_ids=true, to_apply=%add | all-reduce | flops 512 | bytes 2048
  48.2 21.7 %all_gather.43 = bf16[512,768]{1,0:T(8,128)(2,1)S(1)} all-gather(bf16[32,768]{1,0:T(8,128)(2,1)} %param.12), channel_id=1, replica_groups=mesh['ctx_0'=2,'ctx_1'=4,'ctx_2'=2,'vocab_0'=2,'vocab_1'=4] {'ctx_0','ct..., dimensions={0}, use_global_device_ids=true | all-gather | bytes 835584 | tf_op jit(solution)/shard_map/all_gather | solution.py:111
  69.9 0.3 copy.29
  70.3 0.3 select_reduce_fusion.1
  70.6 23.0 %all_gather.44 = bf16[512,768]{1,0:T(8,128)(2,1)S(1)} all-gather(bf16[32,768]{1,0:T(8,128)(2,1)} %param.13), channel_id=1, replica_groups=mesh['ctx_0'=2,'ctx_1'=4,'ctx_2'=2,'vocab_0'=2,'vocab_1'=4] {'ctx_0','ct..., dimensions={0}, use_global_device_ids=true | all-gather | bytes 835584 | tf_op jit(solution)/shard_map/all_gather | solution.py:112
  93.6 0.3 copy.32
  93.9 0.2 fusion.8
  94.1 0.4 fusion.5
  94.6 0.7 convert_element_type.30
  95.2 5.4 %all-to-all-start = ((bf16[8,4,768]{2,1,0:T(4,128)(2,1)}), bf16[8,4,768]{2,1,0:T(4,128)(2,1)S(1)}, u32[]{:S(2)}, u32[]{:S(2)}) async-start(bf16[8,4,768]{2,1,0:T(4,128)(2,1)} %convert_element_type.30), calls=%async_computation | async-start | bytes 98304 | tf_op jit(solution)/shard_map/all_to_all | solution.py:132
  100.8 1.0 copy.48
  102.0 4.9 %all-to-all-done = bf16[8,4,768]{2,1,0:T(4,128)(2,1)S(1)} async-done(((bf16[8,4,768]{2,1,0:T(4,128)(2,1)}), bf16[8,4,768]{2,1,0:T(4,128)(2,1)S(1)}, u32[]{:S(2)}, u32[]{:S(2)}) %all-to-all-start) | async-done | bytes 49184 | tf_op jit(solution)/shard_map/all_to_all | solution.py:132
  107.0 0.5 fusion.61
  107.5 0.5 fusion.10
  108.0 0.6 fusion
  108.6 0.2 multiply_reduce_fusion
  108.9 0.2 multiply_convert_fusion
  109.0 0.1 broadcast_in_dim.61
  109.2 23.8 %all_to_all.18 = bf16[8,16,6144]{2,1,0:T(8,128)(2,1)} all-to-all(bf16[8,16,6144]{2,1,0:T(8,128)(2,1)S(1)} %broadcast_in_dim.61), channel_id=1, replica_groups=mesh['ctx_0'=2,'ctx_1'=4,'ctx_2'=2,'vocab_0'=2,'vocab_1'=4] {'vocab_0','..., dimensions={0} | all-to-all | bytes 3145728 | tf_op jit(solution)/shard_map/all_to_all | solution.py:18
  133.1 0.6 copy_bitcast_fusion
  133.7 143.4 %all-gather.12.cloned.1.call-done = bf16[2048,6144]{1,0:T(8,128)(2,1)} async-done(((bf16[128,6144]{1,0:T(8,128)(2,1)}), bf16[2048,6144]{1,0:T(8,128)(2,1)}) %all-gather.12.cloned.1.call-update) | async-done | bytes 25165840 | tf_op jit(solution)/shard_map/all_gather | solution.py:138
  277.1 34.1 %fusion.62 = (f32[2048]{0:T(1024)S(1)}, f32[2048,1024]{0,1:T(8,128)}) fusion(bf16[2048,6144]{1,0:T(8,128)(2,1)} %all-gather.12.cloned.1.call-done, bf16[6144,1024]{1,0:T(8,128)(2,1)} %param.20), kind=kOutput, calls=%fused_computation.121 | convolution fusion | flops 25771898880 | bytes 46145536 | tf_op jit(solution)/shard_map/dot_general | solution.py:139
  311.2 4.6 %exponential_reduce_fusion = (f32[2048]{0:T(1024)S(1)}, f32[2048]{0:T(1024)S(1)}) fusion(f32[2048,1024]{0,1:T(8,128)} %get-tuple-element.31, f32[2048]{0:T(1024)S(1)} %get-tuple-element.30, s32[2048]{0:T(1024)S(1)} %broadcast_subtract_fusion), kind=kLoop, calls=%fused_computation.2 | loop fusion | flops 10481664 | bytes 8421376 | tf_op jit(solution)/shard_map/reduce_sum | solution.py:141
  315.8 6.1 %all-gather.5 = f32[2,3,2048]{2,1,0:T(4,128)S(1)} all-gather(f32[1,3,2048]{2,1,0:T(4,128)S(1)} %maximum_bitcast_fusion), channel_id=2, replica_groups=mesh['ctx_0'=2,'ctx_1'=4,'ctx_2'=2,'vocab_0'=2,'vocab_1'=4] {'ctx_0'}, dimensions={0}, use_global_device_ids=true | all-gather | bytes 73728 | tf_op jit(solution)/shard_map/all_gather | solution.py:42
  322.0 12.0 %all-gather.6 = f32[4,3,2048]{2,1,0:T(4,128)S(1)} all-gather(f32[1,3,2048]{2,1,0:T(4,128)S(1)} %maximum_bitcast_fusion.1), channel_id=3, replica_groups=mesh['ctx_0'=2,'ctx_1'=4,'ctx_2'=2,'vocab_0'=2,'vocab_1'=4] {'ctx_1'}, dimensions={0}, use_global_device_ids=true | all-gather | bytes 122880 | tf_op jit(solution)/shard_map/all_gather | solution.py:42
  334.2 1.9 all-gather.7
  336.1 4.6 %all-gather.8 = f32[2,3,2048]{2,1,0:T(4,128)S(1)} all-gather(f32[1,3,2048]{2,1,0:T(4,128)S(1)} %maximum_bitcast_fusion.3), channel_id=5, replica_groups=mesh['ctx_0'=2,'ctx_1'=4,'ctx_2'=2,'vocab_0'=2,'vocab_1'=4] {'vocab_0'}, dimensions={0}, use_global_device_ids=true | all-gather | bytes 73728 | tf_op jit(solution)/shard_map/all_gather | solution.py:42
  340.8 12.5 %all-gather.9 = f32[4,3,2048]{2,1,0:T(4,128)S(1)} all-gather(f32[1,3,2048]{2,1,0:T(4,128)S(1)} %maximum_bitcast_fusion.4), channel_id=6, replica_groups=mesh['ctx_0'=2,'ctx_1'=4,'ctx_2'=2,'vocab_0'=2,'vocab_1'=4] {'vocab_1'}, dimensions={0}, use_global_device_ids=true | all-gather | bytes 122880 | tf_op jit(solution)/shard_map/all_gather | solution.py:42
  353.4 0.6 dynamic-slice_subtract_fusion
  (47 shorter events, 1.1 us)
Async XLA Ops:
  7.2 63.1 %copy-start = (bf16[32,768]{1,0:T(8,128)(2,1)S(1)}, bf16[32,768]{1,0:T(8,128)(2,1)}, u32[]{:S(2)}) copy-start(bf16[32,768]{1,0:T(8,128)(2,1)} %param.11) | copy-start | bytes 147460
  7.2 94.6 %copy-start.2 = (bf16[16,6144]{1,0:T(8,128)(2,1)S(1)}, bf16[16,6144]{1,0:T(8,128)(2,1)}, u32[]{:S(2)}) copy-start(bf16[16,6144]{1,0:T(8,128)(2,1)} %param.15) | copy-start | bytes 589828
  7.2 94.7 %copy-start.3 = (bf16[16,6144]{1,0:T(8,128)(2,1)S(1)}, bf16[16,6144]{1,0:T(8,128)(2,1)}, u32[]{:S(2)}) copy-start(bf16[16,6144]{1,0:T(8,128)(2,1)} %param.17) | copy-start | bytes 589828
  69.9 38.7 %copy-start.1 = (bf16[16,6144]{1,0:T(8,128)(2,1)S(1)}, bf16[16,6144]{1,0:T(8,128)(2,1)}, u32[]{:S(2)}) copy-start(bf16[16,6144]{1,0:T(8,128)(2,1)} %param.18) | copy-start | bytes 589828
  70.2 38.7 %copy-start.4 = (f32[6144]{0:T(1024)S(1)}, f32[6144]{0:T(1024)}, u32[]{:S(2)}) copy-start(f32[6144]{0:T(1024)} %param.19) | copy-start | bytes 73732
  95.2 11.7 %all-to-all-start = ((bf16[8,4,768]{2,1,0:T(4,128)(2,1)}), bf16[8,4,768]{2,1,0:T(4,128)(2,1)S(1)}, u32[]{:S(2)}, u32[]{:S(2)}) async-start(bf16[8,4,768]{2,1,0:T(4,128)(2,1)} %convert_element_type.30), calls=%async_computation | async-start | bytes 98304 | tf_op jit(solution)/shard_map/all_to_all | solution.py:132
  100.6 176.4 %all-gather.12.cloned.1.call-start = ((), (), s32[]{:S(2)}) async-start(), calls=%async_computation.2 | async-start | bytes 26738688 | tf_op jit(solution)/shard_map/all_gather | solution.py:138
  101.9 31.2 %copy-start.5 = (s32[2048]{0:T(1024)S(1)}, s32[2048]{0:T(1024)}, u32[]{:S(2)}) copy-start(s32[2048]{0:T(1024)} %param.21) | copy-start | bytes 24580
Sparse Core Ops, SparseCore 0:
  133.2 143.8 all-gather.11
where the time goes:
time: 361 us
  waiting for transfers between devices  148 us (41%)
  blocking collectives  144 us (40%)
  matrix products  35.9 us (10%)
  between operations  15.1 us (4%)
  other arithmetic  7.79 us (2%)
  starting transfers between devices  5.47 us (2%)
  local copies, waits for them, and re-layouts  4.76 us (1%)
    all_gather x1, waiting for transfers between devices, local(): piece = lax.all_gather(group_states, CTX, axis=0, tiled=True)  143 us
    unnamed x1, blocking collectives  38.1 us
    all_gather x5, blocking collectives, all_in_one(): both, at, found = (lax.all_gather(jnp.concatenate(lines), axis), 0, {})  37 us
    dot_general x1, matrix products, local(): logits = jnp.dot(piece, head_weight, preferred_element_type=jnp.float32)  34.1 us
    all_to_all x1, blocking collectives, sent_to_all(): lax.all_to_all(jnp.broadcast_to(value[None], (size, *value.shape)), axis,...  23.8 us
    all_gather x1, blocking collectives, local(): values = lax.all_gather(block_value, CTX, axis=0, tiled=True)  23 us
    all_gather x1, blocking collectives, local(): keys = lax.all_gather(block_key, CTX, axis=0, tiled=True)  21.7 us
  transfers between devices with their start and end apart: 2, of which 2 were waited for; matrix products, arithmetic and copies ran while one was open for 1% of the time, Pallas kernels for 0%

commit v1 on v0

--- a/solution.py
+++ b/solution.py
@@ -108,8 +108,11 @@
     own_doc = block_doc.astype(jnp.bfloat16)
     query_places = first_row + jnp.arange(local_rows, dtype=jnp.int32)
     highest = jnp.full((local_rows, head_count), big_negative, jnp.float32)
-    keys = lax.all_gather(block_key, CTX, axis=0, tiled=True)
-    values = lax.all_gather(block_value, CTX, axis=0, tiled=True)
+    keys, values = jnp.split(
+        lax.all_gather(jnp.concatenate([block_key, block_value], axis=1), CTX, axis=0, tiled=True),
+        [block_key.shape[1]],
+        axis=1,
+    )
     docs = lax.all_gather(own_doc, CTX, axis=0, tiled=True)
     count = keys.shape[0]
     keys = keys.reshape(count, head_count, HEAD_DIM)

time: 361 us -> 330 us (0.914)
  blocking collectives: 144 us -> 98.9 us
  waiting for transfers between devices: 148 us -> 161 us
    all_gather x2 -> x0, blocking collectives: 44.6 us -> none  [the longest x1 23 us: local(): values = lax.all_gather(block_value, CTX, axis=0, tiled=True)]
    all_gather x0 -> x1, waiting for transfers between devices: none -> 9.3 us  [local(): lax.all_gather(jnp.concatenate([block_key, block_value], axis=1), CTX, ax...]
  transfers between devices with their start and end apart: 2 -> 3, of which waited for: 2 -> 3; matrix products, arithmetic and copies ran while one was open for 1% -> 1% of each run, Pallas kernels for 0% -> 0%
where the time goes in v1:
time: 330 us
  waiting for transfers between devices  161 us (49%)
  blocking collectives  98.9 us (30%)
  matrix products  36 us (11%)
  between operations  15.1 us (5%)
  other arithmetic  9.29 us (3%)
  local copies, waits for them, and re-layouts  5.32 us (2%)
  starting transfers between devices  4.53 us (1%)
    all_gather x1, waiting for transfers between devices, local(): piece = lax.all_gather(group_states, CTX, axis=0, tiled=True)  145 us
    unnamed x1, blocking collectives  38.3 us
    all_gather x5, blocking collectives, all_in_one(): both, at, found = (lax.all_gather(jnp.concatenate(lines), axis), 0, {})  37 us
    dot_general x1, matrix products, local(): logits = jnp.dot(piece, head_weight, preferred_element_type=jnp.float32)  34.2 us
    all_to_all x1, blocking collectives, sent_to_all(): lax.all_to_all(jnp.broadcast_to(value[None], (size, *value.shape)), axis,...  23.6 us
    all_gather x1, waiting for transfers between devices, local(): lax.all_gather(jnp.concatenate([block_key, block_value], axis=1), CTX, ax...  9.3 us
  transfers between devices with their start and end apart: 3, of which 3 were waited for; matrix products, arithmetic and copies ran while one was open for 1% of the time, Pallas kernels for 0%

profile of v1, /device:TPU:0, one launch (start us, length us, event | category | flops | bytes accessed | tf_op | source)
XLA Modules:
  0.0 329.7 jit_solution(12721381263863019182)
XLA Ops:
  7.3 1.6 pad_maximum_fusion.4
  8.9 0.7 convert_element_type.25
  9.5 1.2 dynamic-slice
  11.4 0.2 dynamic-update-slice
  11.7 38.3 %all-reduce = bf16[512]{0:T(512)(128)(2,1)S(1)} all-reduce(bf16[512]{0:T(512)(128)(2,1)S(1)} %dynamic-update-slice), channel_id=1, replica_groups=mesh['ctx_0'=2,'ctx_1'=4,'ctx_2'=2,'vocab_0'=2,'vocab_1'=4] {'ctx_0','ct..., use_global_device_ids=true, to_apply=%add | all-reduce | flops 512 | bytes 2048
  50.1 9.3 %all-gather.13.cloned.1.call-done = bf16[512,1536]{1,0:T(8,128)(2,1)} async-done(((bf16[32,1536]{1,0:T(8,128)(2,1)}), bf16[512,1536]{1,0:T(8,128)(2,1)}) %all-gather.13.cloned.1.call-update) | async-done | bytes 1572880 | tf_op jit(solution)/shard_map/all_gather | solution.py:112
  59.4 1.5 fusion.60
  60.9 0.3 copy.46
  61.2 0.3 select_reduce_fusion.1
  61.5 0.3 copy.45
  61.8 0.2 fusion.8
  62.0 0.4 fusion.5
  62.5 0.7 convert_element_type.30
  63.1 4.5 %all-to-all-start = ((bf16[8,4,768]{2,1,0:T(4,128)(2,1)}), bf16[8,4,768]{2,1,0:T(4,128)(2,1)S(1)}, u32[]{:S(2)}, u32[]{:S(2)}) async-start(bf16[8,4,768]{2,1,0:T(4,128)(2,1)} %convert_element_type.30), calls=%async_computation | async-start | bytes 98304 | tf_op jit(solution)/shard_map/all_to_all | solution.py:135
  68.0 5.9 %all-to-all-done = bf16[8,4,768]{2,1,0:T(4,128)(2,1)S(1)} async-done(((bf16[8,4,768]{2,1,0:T(4,128)(2,1)}), bf16[8,4,768]{2,1,0:T(4,128)(2,1)S(1)}, u32[]{:S(2)}, u32[]{:S(2)}) %all-to-all-start) | async-done | bytes 49184 | tf_op jit(solution)/shard_map/all_to_all | solution.py:135
  73.9 0.5 fusion.62
  74.4 0.5 fusion.10
  74.9 0.6 fusion
  75.5 0.2 multiply_reduce_fusion
  75.8 0.2 multiply_convert_fusion
  76.0 0.1 broadcast_in_dim.61
  76.1 23.6 %all_to_all.18 = bf16[8,16,6144]{2,1,0:T(8,128)(2,1)} all-to-all(bf16[8,16,6144]{2,1,0:T(8,128)(2,1)S(1)} %broadcast_in_dim.61), channel_id=1, replica_groups=mesh['ctx_0'=2,'ctx_1'=4,'ctx_2'=2,'vocab_0'=2,'vocab_1'=4] {'vocab_0','..., dimensions={0} | all-to-all | bytes 3145728 | tf_op jit(solution)/shard_map/all_to_all | solution.py:18
  99.8 0.6 copy_bitcast_fusion
  100.4 145.4 %all-gather.15.cloned.1.call-done = bf16[2048,6144]{1,0:T(8,128)(2,1)} async-done(((bf16[128,6144]{1,0:T(8,128)(2,1)}), bf16[2048,6144]{1,0:T(8,128)(2,1)}) %all-gather.15.cloned.1.call-update) | async-done | bytes 25165840 | tf_op jit(solution)/shard_map/all_gather | solution.py:141
  245.8 34.2 %fusion.63 = (f32[2048]{0:T(1024)S(1)}, f32[2048,1024]{0,1:T(8,128)}) fusion(bf16[2048,6144]{1,0:T(8,128)(2,1)} %all-gather.15.cloned.1.call-done, bf16[6144,1024]{1,0:T(8,128)(2,1)} %param.20), kind=kOutput, calls=%fused_computation.123 | convolution fusion | flops 25771898880 | bytes 46145536 | tf_op jit(solution)/shard_map/dot_general | solution.py:142
  280.0 4.6 %exponential_reduce_fusion = (f32[2048]{0:T(1024)S(1)}, f32[2048]{0:T(1024)S(1)}) fusion(f32[2048,1024]{0,1:T(8,128)} %get-tuple-element.33, f32[2048]{0:T(1024)S(1)} %get-tuple-element.32, s32[2048]{0:T(1024)S(1)} %broadcast_subtract_fusion), kind=kLoop, calls=%fused_computation.2 | loop fusion | flops 10481664 | bytes 8421376 | tf_op jit(solution)/shard_map/reduce_sum | solution.py:144
  284.7 6.1 %all-gather.5 = f32[2,3,2048]{2,1,0:T(4,128)S(1)} all-gather(f32[1,3,2048]{2,1,0:T(4,128)S(1)} %maximum_bitcast_fusion), channel_id=2, replica_groups=mesh['ctx_0'=2,'ctx_1'=4,'ctx_2'=2,'vocab_0'=2,'vocab_1'=4] {'ctx_0'}, dimensions={0}, use_global_device_ids=true | all-gather | bytes 73728 | tf_op jit(solution)/shard_map/all_gather | solution.py:42
  290.9 12.0 %all-gather.6 = f32[4,3,2048]{2,1,0:T(4,128)S(1)} all-gather(f32[1,3,2048]{2,1,0:T(4,128)S(1)} %maximum_bitcast_fusion.1), channel_id=3, replica_groups=mesh['ctx_0'=2,'ctx_1'=4,'ctx_2'=2,'vocab_0'=2,'vocab_1'=4] {'ctx_1'}, dimensions={0}, use_global_device_ids=true | all-gather | bytes 122880 | tf_op jit(solution)/shard_map/all_gather | solution.py:42
  303.0 1.9 all-gather.7
  305.0 4.6 %all-gather.8 = f32[2,3,2048]{2,1,0:T(4,128)S(1)} all-gather(f32[1,3,2048]{2,1,0:T(4,128)S(1)} %maximum_bitcast_fusion.3), channel_id=5, replica_groups=mesh['ctx_0'=2,'ctx_1'=4,'ctx_2'=2,'vocab_0'=2,'vocab_1'=4] {'vocab_0'}, dimensions={0}, use_global_device_ids=true | all-gather | bytes 73728 | tf_op jit(solution)/shard_map/all_gather | solution.py:42
  309.7 12.5 %all-gather.9 = f32[4,3,2048]{2,1,0:T(4,128)S(1)} all-gather(f32[1,3,2048]{2,1,0:T(4,128)S(1)} %maximum_bitcast_fusion.4), channel_id=6, replica_groups=mesh['ctx_0'=2,'ctx_1'=4,'ctx_2'=2,'vocab_0'=2,'vocab_1'=4] {'vocab_1'}, dimensions={0}, use_global_device_ids=true | all-gather | bytes 122880 | tf_op jit(solution)/shard_map/all_gather | solution.py:42
  322.3 0.6 dynamic-slice_subtract_fusion
  (52 shorter events, 1.2 us)
Async XLA Ops:
  7.2 54.0 %copy-start = (bf16[32,768]{1,0:T(8,128)(2,1)S(1)}, bf16[32,768]{1,0:T(8,128)(2,1)}, u32[]{:S(2)}) copy-start(bf16[32,768]{1,0:T(8,128)(2,1)} %param.11) | copy-start | bytes 147460
  7.2 60.5 %copy-start.2 = (bf16[16,6144]{1,0:T(8,128)(2,1)S(1)}, bf16[16,6144]{1,0:T(8,128)(2,1)}, u32[]{:S(2)}) copy-start(bf16[16,6144]{1,0:T(8,128)(2,1)} %param.16) | copy-start | bytes 589828
  7.2 60.6 %copy-start.3 = (bf16[16,6144]{1,0:T(8,128)(2,1)S(1)}, bf16[16,6144]{1,0:T(8,128)(2,1)}, u32[]{:S(2)}) copy-start(bf16[16,6144]{1,0:T(8,128)(2,1)} %param.15) | copy-start | bytes 589828
  7.2 60.7 %copy-start.4 = (bf16[16,6144]{1,0:T(8,128)(2,1)S(1)}, bf16[16,6144]{1,0:T(8,128)(2,1)}, u32[]{:S(2)}) copy-start(bf16[16,6144]{1,0:T(8,128)(2,1)} %param.17) | copy-start | bytes 589828
  7.2 52.2 %all-gather.13.cloned.1.call-start = ((), (), s32[]{:S(2)}) async-start(), calls=%async_computation.2 | async-start | bytes 1671168 | tf_op jit(solution)/shard_map/all_gather | solution.py:112
  60.9 14.7 %copy-start.1 = (bf16[16,6144]{1,0:T(8,128)(2,1)S(1)}, bf16[16,6144]{1,0:T(8,128)(2,1)}, u32[]{:S(2)}) copy-start(bf16[16,6144]{1,0:T(8,128)(2,1)} %param.18) | copy-start | bytes 589828
  60.9 14.9 %copy-start.5 = (f32[6144]{0:T(1024)S(1)}, f32[6144]{0:T(1024)}, u32[]{:S(2)}) copy-start(f32[6144]{0:T(1024)} %param.19) | copy-start | bytes 73732
  63.1 10.8 %all-to-all-start = ((bf16[8,4,768]{2,1,0:T(4,128)(2,1)}), bf16[8,4,768]{2,1,0:T(4,128)(2,1)S(1)}, u32[]{:S(2)}, u32[]{:S(2)}) async-start(bf16[8,4,768]{2,1,0:T(4,128)(2,1)} %convert_element_type.30), calls=%async_computation | async-start | bytes 98304 | tf_op jit(solution)/shard_map/all_to_all | solution.py:135
  67.6 178.3 %all-gather.15.cloned.1.call-start = ((), (), s32[]{:S(2)}) async-start(), calls=%async_computation.3 | async-start | bytes 26738688 | tf_op jit(solution)/shard_map/all_gather | solution.py:141
  67.9 31.9 %copy-start.6 = (s32[2048]{0:T(1024)S(1)}, s32[2048]{0:T(1024)}, u32[]{:S(2)}) copy-start(s32[2048]{0:T(1024)} %param.21) | copy-start | bytes 24580
Sparse Core Ops, SparseCore 0:
  10.5 48.8 all-gather.12
  99.9 145.9 all-gather.14
